TPU v7x, 512 devices: a whole 4x4x16 slice. The times are simulated.
512 devices in a mesh: slab: 16 (over z_lo, core), src: 32 (over y, x, z_hi).
Axes of the slice: x: 4, y: 4, z: 16 (z_hi: 2, z_lo: 8; z = z_hi * 8 + z_lo), core: 2. Of those that a mesh axis runs over, the one named last changes fastest.
Arguments:
- trace_values: bfloat16 [32, 8192, 128], P('src', 'slab'), may hold values from -6 to 6
- trace_owner: int32 [32, 8192, 1], P('src', 'slab'), may hold values from 0 to 15; in each aligned block of 512 rows (0 to 511, 512 to 1023, ..., all dimensions but the last counted through in order) at most 64 rows name the same one
- trace_source: int32 [32, 8192], P('src', 'slab'), may hold values from 0 to 511
- source_fields: bfloat16 [2, 8192, 16384], P(None, 'slab', 'src'), may hold values from -0.03125 to 0.03125
- green_fields: bfloat16 [2, 2048, 16384], P(None, 'slab', 'src'), may hold values from -0.0625 to 0.0625
Outputs:
- gradient: float32 [16384], P('src')
Inputs may be any that keep to these rules, and one draw needn't show every extreme that they name: `trace_owner`: among the traces of one device, no owner is named by more than 64 traces, a bound that some block reaches.
All inputs are finite; a program needn't handle non-finite values.
Results may differ from a plain program's by a relative error of at most 0.0026.
Values may be sent and summed in bfloat16 or wider, within the bound.
A program may use at most 64 MiB of HBM per device.

v0:
```python
import jax
import jax.numpy as jnp
from jax import lax
from jax.sharding import PartitionSpec as P


def on_device(trace_values, trace_owner, trace_source, source_fields, green_fields):
    values = trace_values[0]
    owners = trace_owner[0, :, 0]
    locals_id = trace_source[0]
    trace_count = values.shape[0]
    width = values.shape[1]
    half_width = width // 2
    slab_count = lax.axis_size("slab")
    src_count = lax.axis_size("src")
    sources_here = source_fields.shape[1]
    source_ids = jnp.arange(sources_here, dtype=jnp.int32)
    iota_high = (source_ids // 32).astype(jnp.bfloat16)
    iota_low = (source_ids % 32).astype(jnp.bfloat16)
    capacity = 2 * trace_count // slab_count
    owner_hits = (owners[:, None] == jnp.arange(slab_count, dtype=jnp.int32)[None, :]).astype(
        jnp.int32
    )
    ranks = jnp.sum(jnp.cumsum(owner_hits, axis=0) * owner_hits, axis=1) - 1
    slots = owners * capacity + ranks
    placing = (
        jnp.arange(slab_count * capacity, dtype=jnp.int32)[:, None] == slots[None, :]
    ).astype(jnp.bfloat16)
    sent_values = jnp.dot(placing, values, preferred_element_type=jnp.float32).astype(jnp.bfloat16)
    labels = jnp.stack([locals_id // 32 + 1, locals_id % 32 + 1], axis=1).astype(jnp.bfloat16)
    sent_labels = (jnp.dot(placing, labels, preferred_element_type=jnp.float32) - 1.0).astype(
        jnp.bfloat16
    )
    got_values, got_labels = (
        lax.all_to_all(
            sent_values.reshape(slab_count, capacity, width),
            "slab",
            split_axis=0,
            concat_axis=0,
            tiled=True,
        ),
        lax.all_to_all(
            sent_labels.reshape(slab_count, capacity, 2),
            "slab",
            split_axis=0,
            concat_axis=0,
            tiled=True,
        ),
    )
    flat_labels = got_labels.reshape(-1, 2)
    picks = (
        (iota_high[:, None] == flat_labels[None, :, 0])
        & (iota_low[:, None] == flat_labels[None, :, 1])
    ).astype(jnp.bfloat16)
    assembled = jnp.dot(picks, got_values.reshape(-1, width), preferred_element_type=jnp.float32)
    residual_piece = assembled.astype(jnp.bfloat16)
    residual_rows = lax.all_gather(residual_piece, "src", axis=1, tiled=True)
    split_rows = residual_rows.reshape(sources_here, src_count, 2, half_width)
    res_real = split_rows[:, :, 0, :].reshape(sources_here, src_count * half_width)
    res_imag = split_rows[:, :, 1, :].reshape(sources_here, src_count * half_width)
    piece = lax.all_gather(green_fields, "slab", axis=1, tiled=True)
    adj_real = jnp.dot(res_real, piece[0], preferred_element_type=jnp.float32) + jnp.dot(
        res_imag, piece[1], preferred_element_type=jnp.float32
    )
    adj_imag = jnp.dot(res_real, piece[1], preferred_element_type=jnp.float32) - jnp.dot(
        res_imag, piece[0], preferred_element_type=jnp.float32
    )
    adj_real, adj_imag = (adj_real, adj_imag)
    partial_value = jnp.sum(
        source_fields[0].astype(jnp.float32) * adj_real
        - source_fields[1].astype(jnp.float32) * adj_imag,
        axis=0,
    )
    return lax.psum(partial_value, "slab")


def solution(mesh):
    in_specs = (
        P("src", "slab", None),
        P("src", "slab", None),
        P("src", "slab"),
        P(None, "slab", "src"),
        P(None, "slab", "src"),
    )
    out_specs = P("src")
    return jax.shard_map(
        on_device, mesh=mesh, in_specs=in_specs, out_specs=out_specs, check_vma=False
    )
```

profile of v0, /device:TPU:6, one launch (start us, length us, event | category | flops | bytes accessed | tf_op | source)
XLA Modules:
  0.0 432.0 jit_solution(941762704033851159)
XLA Ops:
  6.5 0.0 copy-start
  6.5 0.7 fusion.31
  7.3 1.1 reduce-window.6
  8.4 0.2 slice_reduce_fusion
  8.7 0.8 fusion.30
  9.4 0.7 add_add_fusion
  10.1 0.7 add_convert_fusion
  10.8 0.5 fusion.21
  11.3 0.1 reshape.180
  11.4 0.6 copy.12
  12.0 12.6 %all-to-all-start = ((bf16[16,64,2]{1,2,0:T(2,128)(2,1)}), bf16[16,64,2]{1,2,0:T(2,128)(2,1)S(1)}, u32[]{:S(2)}, u32[]{:S(2)}) async-start(bf16[16,64,2]{1,2,0:T(2,128)(2,1)} %copy.12), calls=%async_computation | async-start | bytes 16384 | tf_op jit(solution)/shard_map/all_to_all | solution.py:42
  24.6 0.0 copy-done
  24.6 1.2 fusion.16
  25.8 9.2 %all-to-all-done = bf16[16,64,2]{1,2,0:T(2,128)(2,1)S(1)} async-done(((bf16[16,64,2]{1,2,0:T(2,128)(2,1)}), bf16[16,64,2]{1,2,0:T(2,128)(2,1)S(1)}, u32[]{:S(2)}, u32[]{:S(2)}) %all-to-all-start) | async-done | bytes 4128 | tf_op jit(solution)/shard_map/all_to_all | solution.py:42
  35.0 3.5 all-to-all-start.1
  38.5 0.0 all-gather.3.cloned.1.call-start
  38.6 0.1 reshape.181
  38.7 14.7 %all-to-all-done.1 = bf16[16,64,128]{2,1,0:T(8,128)(2,1)S(1)} async-done(((bf16[16,64,128]{2,1,0:T(8,128)(2,1)}), bf16[16,64,128]{2,1,0:T(8,128)(2,1)S(1)}, u32[]{:S(2)}, u32[]{:S(2)}) %all-to-all-start.1) | async-done | bytes 262176 | tf_op jit(solution)/shard_map/all_to_all | solution.py:35
  53.4 1.3 fusion.17
  54.7 0.0 all-gather.3.cloned.1.call-update
  54.7 0.0 all-gather.5.cloned.1.call-start
  54.8 0.7 all-gather.5.cloned.1.call-update
  55.5 208.7 %all-gather.3.cloned.1.call-done = bf16[512,4096]{1,0:T(8,128)(2,1)} async-done(((bf16[512,128]{1,0:T(8,128)(2,1)}), bf16[512,4096]{1,0:T(8,128)(2,1)}) %all-gather.3.cloned.1.call-update) | async-done | bytes 4194320 | tf_op jit(solution)/shard_map/all_gather | solution.py:57
  264.2 6.5 %copy.14 = bf16[512,4096]{0,1:T(8,128)(2,1)} copy(bf16[512,4096]{1,0:T(8,128)(2,1)} %all-gather.3.cloned.1.call-done) | data formatting | bytes 8388608 | tf_op jit(solution)/shard_map/all_gather | solution.py:57
  270.7 4.0 fusion.47
  274.7 89.8 %all-gather.5.cloned.1.call-done = bf16[2,2048,512]{2,1,0:T(8,128)(2,1)} async-done(((bf16[2,128,512]{2,1,0:T(8,128)(2,1)}), bf16[2,2048,512]{2,1,0:T(8,128)(2,1)}) %all-gather.5.cloned.1.call-update) | async-done | bytes 4194320 | tf_op jit(solution)/shard_map/all_gather | solution.py:61
  364.5 0.0 copy-start.1
  364.5 3.0 fusion.7
  367.5 0.0 copy-done.1
  367.5 0.0 copy-start.2
  367.5 0.0 copy-start.3
  367.5 3.0 fusion.6
  370.6 0.0 copy-done.2
  370.6 0.1 copy-done.3
  370.6 1.3 fusion.11
  371.9 1.3 fusion.15
  373.2 51.9 %psum.7 = f32[512]{0:T(512)} all-reduce(f32[512]{0:T(512)S(1)} %fusion.15), channel_id=1, replica_groups=mesh['slab'=16,'src'=32] {'slab'}, use_global_device_ids=true, to_apply=%region_4.5 | all-reduce | flops 512 | bytes 4096 | tf_op jit(solution)/shard_map/psum | solution.py:74
  (6 shorter events, 0.1 us)
Async XLA Ops:
  6.5 18.1 %copy-start = (bf16[1,512,128]{2,1,0:T(8,128)(2,1)S(1)}, bf16[1,512,128]{2,1,0:T(8,128)(2,1)}, u32[]{:S(2)}) copy-start(bf16[1,512,128]{2,1,0:T(8,128)(2,1)} %param.5) | copy-start | bytes 393220
  12.0 23.0 %all-to-all-start = ((bf16[16,64,2]{1,2,0:T(2,128)(2,1)}), bf16[16,64,2]{1,2,0:T(2,128)(2,1)S(1)}, u32[]{:S(2)}, u32[]{:S(2)}) async-start(bf16[16,64,2]{1,2,0:T(2,128)(2,1)} %copy.12), calls=%async_computation | async-start | bytes 16384 | tf_op jit(solution)/shard_map/all_to_all | solution.py:42
  35.0 18.5 %all-to-all-start.1 = ((bf16[16,64,128]{2,1,0:T(8,128)(2,1)}), bf16[16,64,128]{2,1,0:T(8,128)(2,1)S(1)}, u32[]{:S(2)}, u32[]{:S(2)}) async-start(bf16[16,64,128]{2,1,0:T(8,128)(2,1)} %bitcast.6), calls=%async_computation.1 | async-start | bytes 524288 | tf_op jit(solution)/shard_map/all_to_all | solution.py:35
  38.5 225.7 %all-gather.3.cloned.1.call-start = ((), (), s32[]{:S(2)}) async-start(), calls=%async_computation.2 | async-start | bytes 4325376 | tf_op jit(solution)/shard_map/all_gather | solution.py:57
  54.7 309.8 %all-gather.5.cloned.1.call-start = ((), (), s32[]{:S(2)}) async-start(), calls=%async_computation.3 | async-start | bytes 4456448 | tf_op jit(solution)/shard_map/all_gather | solution.py:61
  364.5 3.0 copy-start.1
  367.5 3.0 copy-start.2
  367.5 3.1 copy-start.3
Sparse Core Ops, SparseCore 0:
  54.8 209.3 all-gather.2
  266.3 98.1 all-gather.4
where the time goes:
time: 432 us
  waiting for transfers between devices  323 us (75%)
  blocking collectives  51.9 us (12%)
  starting transfers between devices  16.2 us (4%)
  between operations  13.5 us (3%)
  local copies, waits for them, and re-layouts  11.6 us (3%)
  matrix products  11.5 us (3%)
    all_gather x1, waiting for transfers between devices, on_device(): residual_rows = lax.all_gather(residual_piece, 'src', axis=1, tiled=True)  209 us
    all_gather x1, waiting for transfers between devices, on_device(): piece = lax.all_gather(green_fields, 'slab', axis=1, tiled=True)  89.8 us
    psum x1, blocking collectives, on_device(): return lax.psum(partial_value, 'slab')  51.9 us
    all_to_all x1, waiting for transfers between devices, on_device(): lax.all_to_all(sent_values.reshape(slab_count, capacity, width), 'slab',...  14.7 us
    all_to_all x1, starting transfers between devices, on_device(): lax.all_to_all(sent_labels.reshape(slab_count, capacity, 2), 'slab', spli...  12.6 us
    all_to_all x1, waiting for transfers between devices, on_device(): lax.all_to_all(sent_labels.reshape(slab_count, capacity, 2), 'slab', spli...  9.19 us
  transfers between devices with their start and end apart: 4, of which 4 were waited for; matrix products, arithmetic and copies ran while one was open for 3% of the time, Pallas kernels for 0%

commit v1 on v0

--- a/solution.py
+++ b/solution.py
@@ -1,7 +1,24 @@
+import functools
 import jax
 import jax.numpy as jnp
 from jax import lax
 from jax.sharding import PartitionSpec as P
+from jax.lax import all_to_all, axis_size
+
+
+def review_spot_by_axis(frame, mesh_name):
+    return jnp.concatenate(
+        all_to_all(
+            jnp.stack(axis_size(mesh_name) * [frame], axis=0),
+            mesh_name,
+            split_axis=0,
+            concat_axis=0,
+        ),
+        axis=1,
+    )
+
+
+direct_cube_all = functools.partial(review_spot_by_axis, mesh_name="src")
 
 
 def on_device(trace_values, trace_owner, trace_source, source_fields, green_fields):
@@ -54,7 +71,7 @@
     ).astype(jnp.bfloat16)
     assembled = jnp.dot(picks, got_values.reshape(-1, width), preferred_element_type=jnp.float32)
     residual_piece = assembled.astype(jnp.bfloat16)
-    residual_rows = lax.all_gather(residual_piece, "src", axis=1, tiled=True)
+    residual_rows = direct_cube_all(residual_piece)
     split_rows = residual_rows.reshape(sources_here, src_count, 2, half_width)
     res_real = split_rows[:, :, 0, :].reshape(sources_here, src_count * half_width)
     res_imag = split_rows[:, :, 1, :].reshape(sources_here, src_count * half_width)

time: 432 us -> 367 us (0.85)
  waiting for transfers between devices: 323 us -> 245 us
  starting transfers between devices: 16.2 us -> 29.6 us
    all_gather x1 -> x0, waiting for transfers between devices: 209 us -> none  [on_device(): residual_rows = lax.all_gather(residual_piece, 'src', axis=1, tiled=True)]
    all_to_all x0 -> x1, waiting for transfers between devices: none -> 157 us  [review_spot_by_axis(): all_to_all(jnp.stack(axis_size(mesh_name) * [frame], axis=0), mesh_name,...]
    all_gather x1, waiting for transfers between devices: 89.8 us -> 63.1 us  [on_device(): piece = lax.all_gather(green_fields, 'slab', axis=1, tiled=True)]
    all_to_all x0 -> x1, starting transfers between devices: none -> 13.4 us  [review_spot_by_axis(): all_to_all(jnp.stack(axis_size(mesh_name) * [frame], axis=0), mesh_name,...]
    all_gather x1 -> x0, local copies, waits for them, and re-layouts: 6.52 us -> none  [on_device(): residual_rows = lax.all_gather(residual_piece, 'src', axis=1, tiled=True)]
  transfers between devices with their start and end apart: 4 -> 4, of which waited for: 4 -> 4; matrix products, arithmetic and copies ran while one was open for 3% -> 1% of each run, Pallas kernels for 0% -> 0%
where the time goes in v1:
time: 367 us; the launch traced here: 364 us
  waiting for transfers between devices  245 us (67%)
  blocking collectives  53.5 us (15%)
  starting transfers between devices  29.6 us (8%)
  between operations  13.5 us (4%)
  matrix products  10.9 us (3%)
  local copies, waits for them, and re-layouts  7.7 us (2%)
  other arithmetic  4.07 us (1%)
    all_to_all x1, waiting for transfers between devices, review_spot_by_axis(): all_to_all(jnp.stack(axis_size(mesh_name) * [frame], axis=0), mesh_name,...  157 us
    all_gather x1, waiting for transfers between devices, on_device(): piece = lax.all_gather(green_fields, 'slab', axis=1, tiled=True)  63.1 us
    psum x1, blocking collectives, on_device(): return lax.psum(partial_value, 'slab')  53.5 us
    all_to_all x1, waiting for transfers between devices, on_device(): lax.all_to_all(sent_values.reshape(slab_count, capacity, width), 'slab',...  14.8 us
    all_to_all x1, starting transfers between devices, review_spot_by_axis(): all_to_all(jnp.stack(axis_size(mesh_name) * [frame], axis=0), mesh_name,...  13.4 us
    all_to_all x1, starting transfers between devices, on_device(): lax.all_to_all(sent_labels.reshape(slab_count, capacity, 2), 'slab', spli...  12.6 us
    all_to_all x1, waiting for transfers between devices, on_device(): lax.all_to_all(sent_labels.reshape(slab_count, capacity, 2), 'slab', spli...  9.19 us
  transfers between devices with their start and end apart: 4, of which 4 were waited for; matrix products, arithmetic and copies ran while one was open for 1% of the time, Pallas kernels for 0%

profile of v1, /device:TPU:6, one launch (start us, length us, event | category | flops | bytes accessed | tf_op | source)
XLA Modules:
  0.0 363.8 jit_solution(10375588930047333384)
XLA Ops:
  6.5 0.0 copy-start
  6.5 0.7 fusion.31
  7.3 1.1 reduce-window.6
  8.4 0.2 slice_reduce_fusion
  8.7 0.8 fusion.30
  9.4 0.7 add_add_fusion
  10.1 0.7 add_convert_fusion
  10.8 0.5 fusion.21
  11.3 0.1 reshape.182
  11.4 0.6 copy.12
  12.0 12.6 %all-to-all-start = ((bf16[16,64,2]{1,2,0:T(2,128)(2,1)}), bf16[16,64,2]{1,2,0:T(2,128)(2,1)S(1)}, u32[]{:S(2)}, u32[]{:S(2)}) async-start(bf16[16,64,2]{1,2,0:T(2,128)(2,1)} %copy.12), calls=%async_computation | async-start | bytes 16384 | tf_op jit(solution)/shard_map/all_to_all | solution.py:59
  24.6 0.0 copy-done
  24.6 1.2 fusion.16
  25.8 9.2 %all-to-all-done = bf16[16,64,2]{1,2,0:T(2,128)(2,1)S(1)} async-done(((bf16[16,64,2]{1,2,0:T(2,128)(2,1)}), bf16[16,64,2]{1,2,0:T(2,128)(2,1)S(1)}, u32[]{:S(2)}, u32[]{:S(2)}) %all-to-all-start) | async-done | bytes 4128 | tf_op jit(solution)/shard_map/all_to_all | solution.py:59
  35.0 3.5 all-to-all-start.1
  38.5 0.1 reshape.183
  38.7 14.8 %all-to-all-done.1 = bf16[16,64,128]{2,1,0:T(8,128)(2,1)S(1)} async-done(((bf16[16,64,128]{2,1,0:T(8,128)(2,1)}), bf16[16,64,128]{2,1,0:T(8,128)(2,1)S(1)}, u32[]{:S(2)}, u32[]{:S(2)}) %all-to-all-start.1) | async-done | bytes 262176 | tf_op jit(solution)/shard_map/all_to_all | solution.py:52
  53.4 0.6 fusion.17
  54.0 0.1 copy.14
  54.2 2.4 stack.6
  56.6 13.4 %all-to-all-start.2 = ((bf16[32,512,128]{1,2,0:T(8,128)(2,1)}), bf16[32,512,128]{1,2,0:T(8,128)(2,1)}, u32[]{:S(2)}, u32[]{:S(2)}) async-start(bf16[32,512,128]{1,2,0:T(8,128)(2,1)} %stack.6), calls=%async_computation.2 | async-start | bytes 8388608 | tf_op jit(solution)/shard_map/all_to_all | solution.py:11
  70.0 0.0 all-gather.2.cloned.1.call-start
  70.0 0.7 all-gather.2.cloned.1.call-update
  70.7 156.9 %all-to-all-done.2 = bf16[32,512,128]{1,2,0:T(8,128)(2,1)} async-done(((bf16[32,512,128]{1,2,0:T(8,128)(2,1)}), bf16[32,512,128]{1,2,0:T(8,128)(2,1)}, u32[]{:S(2)}, u32[]{:S(2)}) %all-to-all-start.2) | async-done | bytes 4194336 | tf_op jit(solution)/shard_map/all_to_all | solution.py:11
  227.6 4.0 %fusion.47 = (bf16[512,32,1,64]{0,3,2,1:T(8,128)(2,1)}, bf16[512,32,1,64]{0,3,2,1:T(8,128)(2,1)S(1)}) fusion(bf16[512,32,2,64]{0,3,2,1:T(8,128)(2,1)} %bitcast.9), kind=kLoop, calls=%fused_computation.67 | loop fusion | bytes 8388608 | tf_op jit(solution)/shard_map/slice | solution.py:77
  231.6 63.1 %all-gather.2.cloned.1.call-done = bf16[2,2048,512]{2,1,0:T(8,128)(2,1)} async-done(((bf16[2,128,512]{2,1,0:T(8,128)(2,1)}), bf16[2,2048,512]{2,1,0:T(8,128)(2,1)}) %all-gather.2.cloned.1.call-update) | async-done | bytes 4194320 | tf_op jit(solution)/shard_map/all_gather | solution.py:78
  294.7 0.0 copy-start.1
  294.7 3.0 fusion.7
  297.7 0.0 copy-done.1
  297.7 0.0 copy-start.2
  297.8 0.0 copy-start.3
  297.8 3.0 fusion.6
  300.8 0.0 copy-done.2
  300.8 0.1 copy-done.3
  300.9 1.3 fusion.11
  302.1 1.3 fusion.15
  303.5 53.5 %psum.7 = f32[512]{0:T(512)} all-reduce(f32[512]{0:T(512)S(1)} %fusion.15), channel_id=1, replica_groups=mesh['slab'=16,'src'=32] {'slab'}, use_global_device_ids=true, to_apply=%region_4.5 | all-reduce | flops 512 | bytes 4096 | tf_op jit(solution)/shard_map/psum | solution.py:91
  (6 shorter events, 0.1 us)
Async XLA Ops:
  6.5 18.1 %copy-start = (bf16[1,512,128]{2,1,0:T(8,128)(2,1)S(1)}, bf16[1,512,128]{2,1,0:T(8,128)(2,1)}, u32[]{:S(2)}) copy-start(bf16[1,512,128]{2,1,0:T(8,128)(2,1)} %param.5) | copy-start | bytes 393220
  12.0 23.0 %all-to-all-start = ((bf16[16,64,2]{1,2,0:T(2,128)(2,1)}), bf16[16,64,2]{1,2,0:T(2,128)(2,1)S(1)}, u32[]{:S(2)}, u32[]{:S(2)}) async-start(bf16[16,64,2]{1,2,0:T(2,128)(2,1)} %copy.12), calls=%async_computation | async-start | bytes 16384 | tf_op jit(solution)/shard_map/all_to_all | solution.py:59
  35.0 18.5 %all-to-all-start.1 = ((bf16[16,64,128]{2,1,0:T(8,128)(2,1)}), bf16[16,64,128]{2,1,0:T(8,128)(2,1)S(1)}, u32[]{:S(2)}, u32[]{:S(2)}) async-start(bf16[16,64,128]{2,1,0:T(8,128)(2,1)} %bitcast.6), calls=%async_computation.1 | async-start | bytes 524288 | tf_op jit(solution)/shard_map/all_to_all | solution.py:52
  56.6 171.0 %all-to-all-start.2 = ((bf16[32,512,128]{1,2,0:T(8,128)(2,1)}), bf16[32,512,128]{1,2,0:T(8,128)(2,1)}, u32[]{:S(2)}, u32[]{:S(2)}) async-start(bf16[32,512,128]{1,2,0:T(8,128)(2,1)} %stack.6), calls=%async_computation.2 | async-start | bytes 8388608 | tf_op jit(solution)/shard_map/all_to_all | solution.py:11
  70.0 224.7 %all-gather.2.cloned.1.call-start = ((), (), s32[]{:S(2)}) async-start(), calls=%async_computation.3 | async-start | bytes 4456448 | tf_op jit(solution)/shard_map/all_gather | solution.py:78
  294.7 3.0 copy-start.1
  297.7 3.0 copy-start.2
  297.8 3.1 copy-start.3
Sparse Core Ops, SparseCore 0:
  72.9 221.7 all-gather.1

commit v2 on v0

--- a/solution.py
+++ b/solution.py
@@ -71,7 +71,7 @@
         - source_fields[1].astype(jnp.float32) * adj_imag,
         axis=0,
     )
-    return lax.psum(partial_value, "slab")
+    return jnp.sum(jax.lax.all_gather(partial_value, "slab"), axis=0)
 
 
 def solution(mesh):

time: 432 us -> 410 us (0.949)
  blocking collectives: 51.9 us -> 27.7 us
    psum x1 -> x0, blocking collectives: 51.9 us -> none  [on_device(): return lax.psum(partial_value, 'slab')]
    all_gather x0 -> x1, blocking collectives: none -> 27.7 us  [on_device(): return jnp.sum(jax.lax.all_gather(partial_value, 'slab'), axis=0)]
where the time goes in v2:
time: 410 us; the launch traced here: 408 us
  waiting for transfers between devices  323 us (79%)
  blocking collectives  27.7 us (7%)
  starting transfers between devices  16.2 us (4%)
  between operations  13.5 us (3%)
  local copies, waits for them, and re-layouts  11.6 us (3%)
  matrix products  11.5 us (3%)
  other arithmetic  4.69 us (1%)
    all_gather x1, waiting for transfers between devices, on_device(): residual_rows = lax.all_gather(residual_piece, 'src', axis=1, tiled=True)  209 us
    all_gather x1, waiting for transfers between devices, on_device(): piece = lax.all_gather(green_fields, 'slab', axis=1, tiled=True)  89.8 us
    all_gather x1, blocking collectives, on_device(): return jnp.sum(jax.lax.all_gather(partial_value, 'slab'), axis=0)  27.7 us
    all_to_all x1, waiting for transfers between devices, on_device(): lax.all_to_all(sent_values.reshape(slab_count, capacity, width), 'slab',...  14.7 us
    all_to_all x1, starting transfers between devices, on_device(): lax.all_to_all(sent_labels.reshape(slab_count, capacity, 2), 'slab', spli...  12.6 us
    all_to_all x1, waiting for transfers between devices, on_device(): lax.all_to_all(sent_labels.reshape(slab_count, capacity, 2), 'slab', spli...  9.19 us
  transfers between devices with their start and end apart: 4, of which 4 were waited for; matrix products, arithmetic and copies ran while one was open for 3% of the time, Pallas kernels for 0%

profile of v2, /device:TPU:6, one launch (start us, length us, event | category | flops | bytes accessed | tf_op | source)
XLA Modules:
  0.0 408.4 jit_solution(1975520161173682005)
XLA Ops:
  6.5 0.0 copy-start
  6.5 0.7 fusion.31
  7.3 1.1 reduce-window.6
  8.4 0.2 slice_reduce_fusion
  8.7 0.8 fusion.30
  9.4 0.7 add_add_fusion
  10.1 0.7 add_convert_fusion
  10.8 0.5 fusion.21
  11.3 0.1 reshape.180
  11.4 0.6 copy.12
  12.0 12.6 %all-to-all-start = ((bf16[16,64,2]{1,2,0:T(2,128)(2,1)}), bf16[16,64,2]{1,2,0:T(2,128)(2,1)S(1)}, u32[]{:S(2)}, u32[]{:S(2)}) async-start(bf16[16,64,2]{1,2,0:T(2,128)(2,1)} %copy.12), calls=%async_computation | async-start | bytes 16384 | tf_op jit(solution)/shard_map/all_to_all | solution.py:42
  24.6 0.0 copy-done
  24.6 1.2 fusion.16
  25.8 9.2 %all-to-all-done = bf16[16,64,2]{1,2,0:T(2,128)(2,1)S(1)} async-done(((bf16[16,64,2]{1,2,0:T(2,128)(2,1)}), bf16[16,64,2]{1,2,0:T(2,128)(2,1)S(1)}, u32[]{:S(2)}, u32[]{:S(2)}) %all-to-all-start) | async-done | bytes 4128 | tf_op jit(solution)/shard_map/all_to_all | solution.py:42
  35.0 3.5 all-to-all-start.1
  38.5 0.0 all-gather.5.cloned.1.call-start
  38.6 0.1 reshape.181
  38.7 14.7 %all-to-all-done.1 = bf16[16,64,128]{2,1,0:T(8,128)(2,1)S(1)} async-done(((bf16[16,64,128]{2,1,0:T(8,128)(2,1)}), bf16[16,64,128]{2,1,0:T(8,128)(2,1)S(1)}, u32[]{:S(2)}, u32[]{:S(2)}) %all-to-all-start.1) | async-done | bytes 262176 | tf_op jit(solution)/shard_map/all_to_all | solution.py:35
  53.4 1.3 fusion.17
  54.7 0.0 all-gather.5.cloned.1.call-update
  54.7 0.0 all-gather.7.cloned.1.call-start
  54.8 0.7 all-gather.7.cloned.1.call-update
  55.5 208.7 %all-gather.5.cloned.1.call-done = bf16[512,4096]{1,0:T(8,128)(2,1)} async-done(((bf16[512,128]{1,0:T(8,128)(2,1)}), bf16[512,4096]{1,0:T(8,128)(2,1)}) %all-gather.5.cloned.1.call-update) | async-done | bytes 4194320 | tf_op jit(solution)/shard_map/all_gather | solution.py:57
  264.2 6.5 %copy.14 = bf16[512,4096]{0,1:T(8,128)(2,1)} copy(bf16[512,4096]{1,0:T(8,128)(2,1)} %all-gather.5.cloned.1.call-done) | data formatting | bytes 8388608 | tf_op jit(solution)/shard_map/all_gather | solution.py:57
  270.7 4.0 fusion.47
  274.7 89.8 %all-gather.7.cloned.1.call-done = bf16[2,2048,512]{2,1,0:T(8,128)(2,1)} async-done(((bf16[2,128,512]{2,1,0:T(8,128)(2,1)}), bf16[2,2048,512]{2,1,0:T(8,128)(2,1)}) %all-gather.7.cloned.1.call-update) | async-done | bytes 4194320 | tf_op jit(solution)/shard_map/all_gather | solution.py:61
  364.5 0.0 copy-start.1
  364.5 3.0 fusion.7
  367.5 0.0 copy-done.1
  367.5 0.0 copy-start.2
  367.5 0.0 copy-start.3
  367.5 3.0 fusion.6
  370.6 0.0 copy-done.2
  370.6 0.1 copy-done.3
  370.6 1.3 fusion.11
  371.9 1.3 fusion.15
  373.3 27.7 %all-gather.1 = f32[16,1,512]{2,1,0:T(1,128)S(1)} all-gather(f32[1,1,512]{2,1,0:T(1,128)S(1)} %bitcast.84), channel_id=2, replica_groups=mesh['slab'=16,'src'=32] {'slab'}, dimensions={0}, use_global_device_ids=true | all-gather | bytes 34816 | tf_op jit(solution)/shard_map/all_gather | solution.py:74
  400.9 0.6 reduce_sum.29
  (6 shorter events, 0.1 us)
Async XLA Ops:
  6.5 18.1 %copy-start = (bf16[1,512,128]{2,1,0:T(8,128)(2,1)S(1)}, bf16[1,512,128]{2,1,0:T(8,128)(2,1)}, u32[]{:S(2)}) copy-start(bf16[1,512,128]{2,1,0:T(8,128)(2,1)} %param.5) | copy-start | bytes 393220
  12.0 23.0 %all-to-all-start = ((bf16[16,64,2]{1,2,0:T(2,128)(2,1)}), bf16[16,64,2]{1,2,0:T(2,128)(2,1)S(1)}, u32[]{:S(2)}, u32[]{:S(2)}) async-start(bf16[16,64,2]{1,2,0:T(2,128)(2,1)} %copy.12), calls=%async_computation | async-start | bytes 16384 | tf_op jit(solution)/shard_map/all_to_all | solution.py:42
  35.0 18.5 %all-to-all-start.1 = ((bf16[16,64,128]{2,1,0:T(8,128)(2,1)}), bf16[16,64,128]{2,1,0:T(8,128)(2,1)S(1)}, u32[]{:S(2)}, u32[]{:S(2)}) async-start(bf16[16,64,128]{2,1,0:T(8,128)(2,1)} %bitcast.6), calls=%async_computation.1 | async-start | bytes 524288 | tf_op jit(solution)/shard_map/all_to_all | solution.py:35
  38.5 225.7 %all-gather.5.cloned.1.call-start = ((), (), s32[]{:S(2)}) async-start(), calls=%async_computation.2 | async-start | bytes 4325376 | tf_op jit(solution)/shard_map/all_gather | solution.py:57
  54.7 309.8 %all-gather.7.cloned.1.call-start = ((), (), s32[]{:S(2)}) async-start(), calls=%async_computation.3 | async-start | bytes 4456448 | tf_op jit(solution)/shard_map/all_gather | solution.py:61
  364.5 3.0 copy-start.1
  367.5 3.0 copy-start.2
  367.5 3.1 copy-start.3
Sparse Core Ops, SparseCore 0:
  54.8 209.3 all-gather.4
  266.3 98.1 all-gather.6
